TPU v7x, 128 devices: a whole 4x4x4 slice. The times are simulated.
128 devices in a mesh: dp: 16 (over x, y), expert: 8 (over z, core).
Axes of the slice: x: 4, y: 4, z: 4, core: 2. Of those that a mesh axis runs over, the one named last changes fastest.
Arguments:
- context: bfloat16 [8192, 4096], P('dp'), may hold values from -6 to 6
- out_weight: bfloat16 [4096, 4096], P('dp', 'expert'), may hold values from -0.09375 to 0.09375
- residual: bfloat16 [8192, 4096], P('dp', 'expert'), may hold values from -6 to 6
- gate_weight: bfloat16 [8, 4096, 8192], P('expert', None, 'dp'), may hold values from -0.09375 to 0.09375
- up_weight: bfloat16 [8, 4096, 8192], P('expert', None, 'dp'), may hold values from -0.09375 to 0.09375
- down_weight: bfloat16 [8, 8192, 4096], P('expert', 'dp'), may hold values from -0.0625 to 0.0625
- gate_values: float32 [8, 512], P('expert'), may hold values from 0.2 to 1
- chosen_blocks: int32 [8, 4], replicated, may hold values from 0 to 63, as said below
- block_counts: int32 [8], replicated, may hold values from 1 to 4, as said below
Outputs:
- mixed: bfloat16 [8192, 4096], P('dp', 'expert')
Inputs may be any that keep to these rules, and one draw needn't show every extreme that they name: `chosen_blocks`: within one expert the 4 block numbers are distinct; slots from block_counts on are unused but hold valid block numbers. `block_counts`: some expert uses all 4 slots.
All inputs are finite; a program needn't handle non-finite values.
Results may differ from a plain program's by a relative error of at most 0.008.
Values may be sent and summed in bfloat16 or wider, within the bound.
A program may use at most 128 MiB of HBM per device.

v0:
```python
import jax
import jax.numpy as jnp
from jax import lax
from jax.sharding import PartitionSpec as P

BLK = 128
CAP = 4


def body(
    context,
    out_weight,
    residual,
    gate_weight,
    up_weight,
    down_weight,
    gate_values,
    chosen_blocks,
    block_counts,
):
    n_dp = lax.axis_size("dp")
    n_expert = lax.axis_size("expert")
    local_tokens = context.shape[0]
    local_width = residual.shape[1]
    model_width = context.shape[1]
    local_blocks = local_tokens // BLK
    n_blocks = local_blocks * n_dp
    piece = BLK // n_dp
    my_expert = lax.axis_index("expert")
    projected = jnp.dot(
        context,
        lax.all_gather(out_weight, "dp", axis=0, tiled=True),
        preferred_element_type=jnp.float32,
    )
    attended = (residual.astype(jnp.float32) + projected).astype(jnp.bfloat16)
    split = attended.reshape(local_blocks, n_dp, piece, local_width).transpose(1, 0, 2, 3)
    pieces = lax.all_to_all(split, "dp", 0, 0, tiled=True)
    pieces = pieces.reshape(n_blocks, piece, local_width)
    slots = jnp.take(pieces, chosen_blocks.reshape(-1), axis=0)
    slots = slots.reshape(n_expert, CAP, piece, local_width)
    mine = lax.all_to_all(slots, "expert", 0, 3, tiled=True)
    mine = mine.reshape(CAP * piece, model_width)
    picked = lax.all_gather(mine, "dp", axis=0, tiled=True)
    w_gate = gate_weight[0]
    w_up = up_weight[0]
    w_down = down_weight[0]
    gate_row = gate_values[0]
    my_count = lax.dynamic_index_in_dim(block_counts, my_expert, 0, keepdims=False)
    live = jnp.arange(CAP * BLK) // BLK < my_count
    scale = jnp.where(live, gate_row, jnp.zeros_like(gate_row))
    scale = scale.reshape(CAP, n_dp, piece).transpose(1, 0, 2).reshape(-1)
    gate = jnp.dot(picked, w_gate, preferred_element_type=jnp.float32)
    upper = jnp.dot(picked, w_up, preferred_element_type=jnp.float32)
    hidden = (jax.nn.silu(gate) * upper).astype(jnp.bfloat16)
    part = jnp.dot(hidden, w_down, preferred_element_type=jnp.float32)
    part = (part * scale[:, None]).astype(jnp.bfloat16)
    summed = lax.psum_scatter(
        part.reshape(n_dp, CAP * piece, model_width), "dp", scatter_dimension=0, tiled=True
    )
    summed = summed.reshape(CAP * piece, n_expert, local_width).transpose(1, 0, 2)
    outs = lax.all_to_all(summed, "expert", 0, 0, tiled=True)
    outs = outs.reshape(n_expert * CAP, piece * local_width)
    selector = chosen_blocks.reshape(-1)[None, :] == jnp.arange(n_blocks)[:, None]
    added = jnp.dot(selector.astype(jnp.bfloat16), outs, preferred_element_type=jnp.float32)
    added = added.reshape(n_dp, local_blocks, piece, local_width)
    back = lax.all_to_all(added, "dp", 0, 0, tiled=True)
    back = back.transpose(1, 0, 2, 3).reshape(local_tokens, local_width)
    total = attended.astype(jnp.float32) + back
    return total.astype(jnp.bfloat16)


def solution(mesh):
    in_specs = (
        P("dp", None),
        P("dp", "expert"),
        P("dp", "expert"),
        P("expert", None, "dp"),
        P("expert", None, "dp"),
        P("expert", "dp", None),
        P("expert", None),
        P(),
        P(),
    )
    out_specs = P("dp", "expert")
    return jax.shard_map(body, mesh=mesh, in_specs=in_specs, out_specs=out_specs, check_vma=False)
```

profile of v0, /device:TPU:0, one launch (start us, length us, event | category | flops | bytes accessed | tf_op | source)
XLA Modules:
  0.0 281.9 jit_solution(4458407969886781237)
XLA Ops:
  6.5 0.7 all-gather.3.cloned.1.call-update
  7.3 0.8 copy.29
  8.1 55.3 %all-gather.3.cloned.1.call-done = bf16[4096,512]{1,0:T(8,128)(2,1)} async-done(((bf16[256,512]{1,0:T(8,128)(2,1)}), bf16[4096,512]{1,0:T(8,128)(2,1)}) %all-gather.3.cloned.1.call-update) | async-done | bytes 4194320 | tf_op jit(solution)/shard_map/all_gather | solution.py:32
  63.4 5.8 %fusion.8 = bf16[512,512]{1,0:T(8,128)(2,1)S(1)} fusion(bf16[512,4096]{1,0:T(8,128)(2,1)} %param.9, bf16[4096,512]{1,0:T(8,128)(2,1)} %all-gather.3.cloned.1.call-done, bf16[512,512]{1,0:T(8,128)(2,1)} %param.11), kind=kOutput, calls=%fused_computation.9 | convolution fusion | flops 2148270080 | bytes 9437184 | tf_op jit(solution)/shard_map/dot_general | solution.py:30
  69.3 0.8 copy.49
  70.1 5.3 %all-to-all-start = ((bf16[16,4,8,512]{3,2,1,0:T(8,128)(2,1)}), bf16[16,4,8,512]{3,2,1,0:T(8,128)(2,1)S(1)}, u32[]{:S(2)}, u32[]{:S(2)}) async-start(bf16[16,4,8,512]{3,2,1,0:T(8,128)(2,1)} %bitcast.60), calls=%async_computation | async-start | bytes 1048576 | tf_op jit(solution)/shard_map/all_to_all | solution.py:37
  75.5 0.1 copy.30
  75.6 11.3 %all-to-all-done = bf16[16,4,8,512]{3,2,1,0:T(8,128)(2,1)S(1)} async-done(((bf16[16,4,8,512]{3,2,1,0:T(8,128)(2,1)}), bf16[16,4,8,512]{3,2,1,0:T(8,128)(2,1)S(1)}, u32[]{:S(2)}, u32[]{:S(2)}) %all-to-all-start) | async-done | bytes 524320 | tf_op jit(solution)/shard_map/all_to_all | solution.py:37
  86.9 0.6 gather_fusion
  87.4 0.1 broadcast_select_fusion
  87.6 11.8 %all_to_all.30 = bf16[8,4,8,512]{3,2,1,0:T(8,128)(2,1)S(1)} all-to-all(bf16[8,4,8,512]{3,2,1,0:T(8,128)(2,1)S(1)} %broadcast_select_fusion), channel_id=1, replica_groups=mesh['dp'=16,'expert'=8] {'expert'}, dimensions={0} | all-to-all | bytes 524288 | tf_op jit(solution)/shard_map/all_to_all | solution.py:41
  99.3 0.1 copy.50
  99.5 0.8 copy.41
  100.3 0.6 broadcast.96
  100.9 0.7 reduce.3
  101.7 0.7 dynamic_slice.4
  102.4 0.7 select_bitcast_fusion
  103.1 0.1 mul.19
  103.2 44.6 %all-gather.5.cloned.1.call-done = bf16[512,4096]{1,0:T(8,128)(2,1)} async-done(((bf16[32,4096]{1,0:T(8,128)(2,1)}), bf16[512,4096]{1,0:T(8,128)(2,1)}) %all-gather.5.cloned.1.call-update) | async-done | bytes 4194320 | tf_op jit(solution)/shard_map/all_gather | solution.py:43
  147.8 5.9 %fusion.3 = f32[512,512]{1,0:T(8,128)S(1)} fusion(bf16[512,4096]{1,0:T(8,128)(2,1)} %all-gather.5.cloned.1.call-done, bf16[1,4096,512]{2,1,0:T(8,128)(2,1)} %param.12), kind=kOutput, calls=%fused_computation.5 | convolution fusion | flops 2147483648 | bytes 9437184 | tf_op jit(solution)/shard_map/dot_general | solution.py:52
  153.8 2.4 fusion.9
  156.2 4.3 %multiply_convert_fusion = bf16[512,4096]{1,0:T(8,128)(2,1)} fusion(bf16[512,512]{1,0:T(8,128)(2,1)S(1)} %fusion.9, bf16[1,512,4096]{2,1,0:T(8,128)(2,1)S(1)} %copy-done.3, f32[512]{0:T(512)S(1)} %mul.19), kind=kOutput, calls=%fused_computation.1 | convolution fusion | flops 2151677952 | bytes 8914944 | tf_op jit(solution)/shard_map/dot_general | solution.py:55
  160.6 77.4 %reduce-scatter.4.cloned.1.call-done = bf16[1,32,4096]{2,1,0:T(8,128)(2,1)} async-done(((bf16[16,32,4096]{2,1,0:T(8,128)(2,1)}), bf16[1,32,4096]{2,1,0:T(8,128)(2,1)}) %reduce-scatter.4.cloned.1.call-update) | async-done | bytes 262160
  237.9 1.0 copy.42
  239.0 0.8 copy.35
  239.7 4.4 %all-to-all-start.2 = ((bf16[8,32,512]{2,1,0:T(8,128)(2,1)}), bf16[8,32,512]{2,1,0:T(8,128)(2,1)S(1)}, u32[]{:S(2)}, u32[]{:S(2)}) async-start(bf16[8,32,512]{2,1,0:T(8,128)(2,1)} %copy.35), calls=%async_computation.2 | async-start | bytes 524288 | tf_op jit(solution)/shard_map/all_to_all | solution.py:61
  244.2 7.5 %all-to-all-done.2 = bf16[8,32,512]{2,1,0:T(8,128)(2,1)S(1)} async-done(((bf16[8,32,512]{2,1,0:T(8,128)(2,1)}), bf16[8,32,512]{2,1,0:T(8,128)(2,1)S(1)}, u32[]{:S(2)}, u32[]{:S(2)}) %all-to-all-start.2) | async-done | bytes 262176 | tf_op jit(solution)/shard_map/all_to_all | solution.py:61
  251.7 0.1 reshape.99
  251.8 0.3 fusion.13
  252.1 0.6 copy.37
  252.8 21.5 %all_to_all.31 = f32[16,4,8,512]{3,2,1,0:T(8,128)S(1)} all-to-all(f32[16,4,8,512]{3,2,1,0:T(8,128)S(1)} %copy.37), channel_id=1, replica_groups=mesh['dp'=16,'expert'=8] {'dp'}, dimensions={0} | all-to-all | bytes 2097152 | tf_op jit(solution)/shard_map/all_to_all | solution.py:66
  274.3 1.0 fusion.12
  (26 shorter events, 0.5 us)
Async XLA Ops:
  6.5 56.9 %all-gather.3.cloned.1.call-start = ((), (), s32[]{:S(2)}) async-start(), calls=%async_computation.5 | async-start | bytes 4456448 | tf_op jit(solution)/shard_map/all_gather | solution.py:32
  8.1 67.3 %copy-start = (s32[8,4]{0,1:T(4,128)S(1)}, s32[8,4]{0,1:T(4,128)}, u32[]{:S(2)}) copy-start(s32[8,4]{0,1:T(4,128)} %param.16) | copy-start | bytes 388
  69.2 31.7 %copy-start.1 = (f32[1,512]{1,0:T(1,128)S(1)}, f32[1,512]{1,0:T(1,128)}, u32[]{:S(2)}) copy-start(f32[1,512]{1,0:T(1,128)} %param.15) | copy-start | bytes 6148
  69.3 32.4 %copy-start.5 = (s32[8]{0:T(128)S(1)}, s32[8]{0:T(128)}, u32[]{:S(2)}) copy-start(s32[8]{0:T(128)} %param.17) | copy-start | bytes 100
  70.1 16.8 %all-to-all-start = ((bf16[16,4,8,512]{3,2,1,0:T(8,128)(2,1)}), bf16[16,4,8,512]{3,2,1,0:T(8,128)(2,1)S(1)}, u32[]{:S(2)}, u32[]{:S(2)}) async-start(bf16[16,4,8,512]{3,2,1,0:T(8,128)(2,1)} %bitcast.60), calls=%async_computation | async-start | bytes 1048576 | tf_op jit(solution)/shard_map/all_to_all | solution.py:37
  75.4 72.4 %all-gather.5.cloned.1.call-start = ((), (), s32[]{:S(2)}) async-start(), calls=%async_computation.6 | async-start | bytes 4456448 | tf_op jit(solution)/shard_map/all_gather | solution.py:43
  100.3 137.6 %reduce-scatter.4.cloned.1.call-start = ((), (), s32[]{:S(2)}) async-start(), calls=%async_computation.7 | async-start | bytes 4456448
  147.8 5.9 %copy-start.2 = (bf16[1,4096,512]{2,1,0:T(8,128)(2,1)S(1)}, bf16[1,4096,512]{2,1,0:T(8,128)(2,1)}, u32[]{:S(2)}) copy-start(bf16[1,4096,512]{2,1,0:T(8,128)(2,1)} %param.13) | copy-start | bytes 12582916
  147.8 5.9 %copy-start.4 = (bf16[512,4096]{1,0:T(8,128)(2,1)S(1)}, bf16[512,4096]{1,0:T(8,128)(2,1)}, u32[]{:S(2)}) copy-start(bf16[512,4096]{1,0:T(8,128)(2,1)} %all-gather.5.cloned.1.call-done) | copy-start | bytes 12582916
  153.8 2.5 copy-start.3
  239.7 11.9 %all-to-all-start.2 = ((bf16[8,32,512]{2,1,0:T(8,128)(2,1)}), bf16[8,32,512]{2,1,0:T(8,128)(2,1)S(1)}, u32[]{:S(2)}, u32[]{:S(2)}) async-start(bf16[8,32,512]{2,1,0:T(8,128)(2,1)} %copy.35), calls=%async_computation.2 | async-start | bytes 524288 | tf_op jit(solution)/shard_map/all_to_all | solution.py:61
Sparse Core Ops, SparseCore 0:
  9.5 53.8 all-gather.2
  100.4 47.3 all-gather.4
  160.7 77.1 reduce-scatter.3
where the time goes:
time: 282 us
  waiting for transfers between devices  197 us (70%)
  blocking collectives  33.3 us (12%)
  matrix products  18.9 us (7%)
  between operations  13.3 us (5%)
  starting transfers between devices  9.73 us (3%)
  local copies, waits for them, and re-layouts  7.46 us (3%)
    unnamed x4, waiting for transfers between devices  78.1 us
    all_gather x1, waiting for transfers between devices, body(): lax.all_gather(out_weight, 'dp', axis=0, tiled=True)  55.3 us
    all_gather x1, waiting for transfers between devices, body(): picked = lax.all_gather(mine, 'dp', axis=0, tiled=True)  44.6 us
    all_to_all x1, blocking collectives, body(): back = lax.all_to_all(added, 'dp', 0, 0, tiled=True)  21.5 us
    all_to_all x1, blocking collectives, body(): mine = lax.all_to_all(slots, 'expert', 0, 3, tiled=True)  11.8 us
    all_to_all x1, waiting for transfers between devices, body(): pieces = lax.all_to_all(split, 'dp', 0, 0, tiled=True)  11.3 us
    all_to_all x1, waiting for transfers between devices, body(): outs = lax.all_to_all(summed, 'expert', 0, 0, tiled=True)  7.45 us
    dot_general x1, matrix products, body(): gate = jnp.dot(picked, w_gate, preferred_element_type=jnp.float32)  5.92 us
  transfers between devices with their start and end apart: 5, of which 5 were waited for; matrix products, arithmetic and copies ran while one was open for 1% of the time, Pallas kernels for 0%

commit v1 on v0

--- a/solution.py
+++ b/solution.py
@@ -40,7 +40,9 @@
     slots = slots.reshape(n_expert, CAP, piece, local_width)
     mine = lax.all_to_all(slots, "expert", 0, 3, tiled=True)
     mine = mine.reshape(CAP * piece, model_width)
-    picked = lax.all_gather(mine, "dp", axis=0, tiled=True)
+    picked = jnp.concatenate(
+        lax.all_to_all(jnp.stack([mine] * lax.axis_size("dp")), "dp", 0, 0), axis=0
+    )
     w_gate = gate_weight[0]
     w_up = up_weight[0]
     w_down = down_weight[0]

time: 282 us -> 309 us (1.096)
  waiting for transfers between devices: 197 us -> 214 us
  starting transfers between devices: 9.73 us -> 14.4 us
    all_to_all x0 -> x1, waiting for transfers between devices: none -> 59.7 us  [body(): lax.all_to_all(jnp.stack([mine] * lax.axis_size('dp')), 'dp', 0, 0)]
    all_gather x1 -> x0, waiting for transfers between devices: 44.6 us -> none  [body(): picked = lax.all_gather(mine, 'dp', axis=0, tiled=True)]
    all_to_all x0 -> x1, starting transfers between devices: none -> 4.68 us  [body(): lax.all_to_all(jnp.stack([mine] * lax.axis_size('dp')), 'dp', 0, 0)]
    unnamed x4 -> x3, waiting for transfers between devices: 78.1 us -> 80.7 us
where the time goes in v1:
time: 309 us; the launch traced here: 308 us
  waiting for transfers between devices  214 us (69%)
  blocking collectives  33.2 us (11%)
  matrix products  21.2 us (7%)
  starting transfers between devices  14.4 us (5%)
  between operations  13.6 us (4%)
  local copies, waits for them, and re-layouts  9.09 us (3%)
    unnamed x3, waiting for transfers between devices  80.7 us
    all_to_all x1, waiting for transfers between devices, body(): lax.all_to_all(jnp.stack([mine] * lax.axis_size('dp')), 'dp', 0, 0)  59.7 us
    all_gather x1, waiting for transfers between devices, body(): lax.all_gather(out_weight, 'dp', axis=0, tiled=True)  55.3 us
    all_to_all x1, blocking collectives, body(): back = lax.all_to_all(added, 'dp', 0, 0, tiled=True)  21.5 us
    all_to_all x1, blocking collectives, body(): mine = lax.all_to_all(slots, 'expert', 0, 3, tiled=True)  11.8 us
    all_to_all x1, waiting for transfers between devices, body(): pieces = lax.all_to_all(split, 'dp', 0, 0, tiled=True)  11.4 us
    all_to_all x1, waiting for transfers between devices, body(): outs = lax.all_to_all(summed, 'expert', 0, 0, tiled=True)  7.45 us
  transfers between devices with their start and end apart: 5, of which 5 were waited for; matrix products, arithmetic and copies ran while one was open for 1% of the time, Pallas kernels for 0%

profile of v1, /device:TPU:0, one launch (start us, length us, event | category | flops | bytes accessed | tf_op | source)
XLA Modules:
  0.0 308.4 jit_solution(16790370662543826187)
XLA Ops:
  6.5 0.7 all-gather.2.cloned.1.call-update
  7.3 0.8 copy.29
  8.1 55.3 %all-gather.2.cloned.1.call-done = bf16[4096,512]{1,0:T(8,128)(2,1)} async-done(((bf16[256,512]{1,0:T(8,128)(2,1)}), bf16[4096,512]{1,0:T(8,128)(2,1)}) %all-gather.2.cloned.1.call-update) | async-done | bytes 4194320 | tf_op jit(solution)/shard_map/all_gather | solution.py:32
  63.4 5.9 %fusion.8 = bf16[512,512]{1,0:T(8,128)(2,1)S(1)} fusion(bf16[512,4096]{1,0:T(8,128)(2,1)} %param.9, bf16[4096,512]{1,0:T(8,128)(2,1)} %all-gather.2.cloned.1.call-done, bf16[512,512]{1,0:T(8,128)(2,1)} %param.11), kind=kOutput, calls=%fused_computation.9 | convolution fusion | flops 2148270080 | bytes 9437184 | tf_op jit(solution)/shard_map/dot_general | solution.py:30
  69.3 0.8 copy.49
  70.1 5.3 %all-to-all-start = ((bf16[16,4,8,512]{3,2,1,0:T(8,128)(2,1)}), bf16[16,4,8,512]{3,2,1,0:T(8,128)(2,1)S(1)}, u32[]{:S(2)}, u32[]{:S(2)}) async-start(bf16[16,4,8,512]{3,2,1,0:T(8,128)(2,1)} %bitcast.61), calls=%async_computation | async-start | bytes 1048576 | tf_op jit(solution)/shard_map/all_to_all | solution.py:37
  75.5 11.4 %all-to-all-done = bf16[16,4,8,512]{3,2,1,0:T(8,128)(2,1)S(1)} async-done(((bf16[16,4,8,512]{3,2,1,0:T(8,128)(2,1)}), bf16[16,4,8,512]{3,2,1,0:T(8,128)(2,1)S(1)}, u32[]{:S(2)}, u32[]{:S(2)}) %all-to-all-start) | async-done | bytes 524320 | tf_op jit(solution)/shard_map/all_to_all | solution.py:37
  86.9 0.6 gather_fusion
  87.4 0.1 broadcast_select_fusion
  87.5 11.8 %all_to_all.35 = bf16[8,4,8,512]{3,2,1,0:T(8,128)(2,1)S(1)} all-to-all(bf16[8,4,8,512]{3,2,1,0:T(8,128)(2,1)S(1)} %broadcast_select_fusion), channel_id=1, replica_groups=mesh['dp'=16,'expert'=8] {'expert'}, dimensions={0} | all-to-all | bytes 524288 | tf_op jit(solution)/shard_map/all_to_all | solution.py:41
  99.3 0.1 copy.50
  99.6 2.5 stack.3
  102.0 4.7 %all-to-all-start.2 = ((bf16[16,32,4096]{2,1,0:T(8,128)(2,1)}), bf16[16,32,4096]{2,1,0:T(8,128)(2,1)}, u32[]{:S(2)}, u32[]{:S(2)}) async-start(bf16[16,32,4096]{2,1,0:T(8,128)(2,1)} %stack.3), calls=%async_computation.2 | async-start | bytes 8388608 | tf_op jit(solution)/shard_map/all_to_all | solution.py:44
  106.8 0.5 broadcast.97
  107.3 0.7 reduce.3
  108.1 0.6 dynamic_slice.4
  108.7 0.7 select_bitcast_fusion
  109.4 0.1 mul.19
  109.5 59.7 %all-to-all-done.2 = bf16[16,32,4096]{2,1,0:T(8,128)(2,1)} async-done(((bf16[16,32,4096]{2,1,0:T(8,128)(2,1)}), bf16[16,32,4096]{2,1,0:T(8,128)(2,1)}, u32[]{:S(2)}, u32[]{:S(2)}) %all-to-all-start.2) | async-done | bytes 4194336 | tf_op jit(solution)/shard_map/all_to_all | solution.py:44
  169.1 5.9 %fusion.3 = f32[512,512]{1,0:T(8,128)S(1)} fusion(bf16[512,4096]{1,0:T(8,128)(2,1)} %bitcast.9, bf16[1,4096,512]{2,1,0:T(8,128)(2,1)} %param.12), kind=kOutput, calls=%fused_computation.5 | convolution fusion | flops 2147483648 | bytes 9437184 | tf_op jit(solution)/shard_map/dot_general | solution.py:54
  175.1 4.8 %fusion.9 = bf16[512,512]{1,0:T(8,128)(2,1)S(1)} fusion(bf16[512,4096]{1,0:T(8,128)(2,1)} %bitcast.9, bf16[1,4096,512]{2,1,0:T(8,128)(2,1)S(1)} %copy-done.2, f32[512,512]{1,0:T(8,128)S(1)} %fusion.3), kind=kOutput, calls=%fused_computation.10 | convolution fusion | flops 2149056512 | bytes 9961472 | tf_op jit(solution)/shard_map/dot_general | solution.py:55
  179.9 4.3 %multiply_convert_fusion = bf16[512,4096]{1,0:T(8,128)(2,1)} fusion(bf16[512,512]{1,0:T(8,128)(2,1)S(1)} %fusion.9, bf16[1,512,4096]{2,1,0:T(8,128)(2,1)S(1)} %copy-done.3, f32[512]{0:T(512)S(1)} %mul.19), kind=kOutput, calls=%fused_computation.1 | convolution fusion | flops 2151677952 | bytes 8914944 | tf_op jit(solution)/shard_map/dot_general | solution.py:57
  184.2 79.9 %reduce-scatter.4.cloned.1.call-done = bf16[1,32,4096]{2,1,0:T(8,128)(2,1)} async-done(((bf16[16,32,4096]{2,1,0:T(8,128)(2,1)}), bf16[1,32,4096]{2,1,0:T(8,128)(2,1)}) %reduce-scatter.4.cloned.1.call-update) | async-done | bytes 262160
  264.1 1.0 copy.42
  265.2 0.8 copy.35
  266.0 4.4 %all-to-all-start.3 = ((bf16[8,32,512]{2,1,0:T(8,128)(2,1)}), bf16[8,32,512]{2,1,0:T(8,128)(2,1)S(1)}, u32[]{:S(2)}, u32[]{:S(2)}) async-start(bf16[8,32,512]{2,1,0:T(8,128)(2,1)} %copy.35), calls=%async_computation.3 | async-start | bytes 524288 | tf_op jit(solution)/shard_map/all_to_all | solution.py:63
  270.5 7.5 %all-to-all-done.3 = bf16[8,32,512]{2,1,0:T(8,128)(2,1)S(1)} async-done(((bf16[8,32,512]{2,1,0:T(8,128)(2,1)}), bf16[8,32,512]{2,1,0:T(8,128)(2,1)S(1)}, u32[]{:S(2)}, u32[]{:S(2)}) %all-to-all-start.3) | async-done | bytes 262176 | tf_op jit(solution)/shard_map/all_to_all | solution.py:63
  277.9 0.1 reshape.101
  278.1 0.3 fusion.13
  278.4 0.6 copy.37
  279.0 21.5 %all_to_all.36 = f32[16,4,8,512]{3,2,1,0:T(8,128)S(1)} all-to-all(f32[16,4,8,512]{3,2,1,0:T(8,128)S(1)} %copy.37), channel_id=1, replica_groups=mesh['dp'=16,'expert'=8] {'dp'}, dimensions={0} | all-to-all | bytes 2097152 | tf_op jit(solution)/shard_map/all_to_all | solution.py:68
  300.6 1.0 fusion.12
  (24 shorter events, 0.6 us)
Async XLA Ops:
  6.5 56.9 %all-gather.2.cloned.1.call-start = ((), (), s32[]{:S(2)}) async-start(), calls=%async_computation.6 | async-start | bytes 4456448 | tf_op jit(solution)/shard_map/all_gather | solution.py:32
  8.1 67.3 %copy-start = (s32[8,4]{0,1:T(4,128)S(1)}, s32[8,4]{0,1:T(4,128)}, u32[]{:S(2)}) copy-start(s32[8,4]{0,1:T(4,128)} %param.16) | copy-start | bytes 388
  70.1 16.8 %all-to-all-start = ((bf16[16,4,8,512]{3,2,1,0:T(8,128)(2,1)}), bf16[16,4,8,512]{3,2,1,0:T(8,128)(2,1)S(1)}, u32[]{:S(2)}, u32[]{:S(2)}) async-start(bf16[16,4,8,512]{3,2,1,0:T(8,128)(2,1)} %bitcast.61), calls=%async_computation | async-start | bytes 1048576 | tf_op jit(solution)/shard_map/all_to_all | solution.py:37
  102.0 5.3 %copy-start.1 = (f32[1,512]{1,0:T(1,128)S(1)}, f32[1,512]{1,0:T(1,128)}, u32[]{:S(2)}) copy-start(f32[1,512]{1,0:T(1,128)} %param.15) | copy-start | bytes 6148
  102.0 6.0 %copy-start.4 = (s32[8]{0:T(128)S(1)}, s32[8]{0:T(128)}, u32[]{:S(2)}) copy-start(s32[8]{0:T(128)} %param.17) | copy-start | bytes 100
  102.0 67.1 %all-to-all-start.2 = ((bf16[16,32,4096]{2,1,0:T(8,128)(2,1)}), bf16[16,32,4096]{2,1,0:T(8,128)(2,1)}, u32[]{:S(2)}, u32[]{:S(2)}) async-start(bf16[16,32,4096]{2,1,0:T(8,128)(2,1)} %stack.3), calls=%async_computation.2 | async-start | bytes 8388608 | tf_op jit(solution)/shard_map/all_to_all | solution.py:44
  106.7 157.4 %reduce-scatter.4.cloned.1.call-start = ((), (), s32[]{:S(2)}) async-start(), calls=%async_computation.7 | async-start | bytes 4456448
  169.1 5.9 %copy-start.2 = (bf16[1,4096,512]{2,1,0:T(8,128)(2,1)S(1)}, bf16[1,4096,512]{2,1,0:T(8,128)(2,1)}, u32[]{:S(2)}) copy-start(bf16[1,4096,512]{2,1,0:T(8,128)(2,1)} %param.13) | copy-start | bytes 12582916
  175.1 4.8 %copy-start.3 = (bf16[1,512,4096]{2,1,0:T(8,128)(2,1)S(1)}, bf16[1,512,4096]{2,1,0:T(8,128)(2,1)}, u32[]{:S(2)}) copy-start(bf16[1,512,4096]{2,1,0:T(8,128)(2,1)} %param.14) | copy-start | bytes 12582916
  266.0 12.0 %all-to-all-start.3 = ((bf16[8,32,512]{2,1,0:T(8,128)(2,1)}), bf16[8,32,512]{2,1,0:T(8,128)(2,1)S(1)}, u32[]{:S(2)}, u32[]{:S(2)}) async-start(bf16[8,32,512]{2,1,0:T(8,128)(2,1)} %copy.35), calls=%async_computation.3 | async-start | bytes 524288 | tf_op jit(solution)/shard_map/all_to_all | solution.py:63
Sparse Core Ops, SparseCore 0:
  9.5 53.8 all-gather.1
  184.3 79.7 reduce-scatter.3
